TPU v7x, 128 devices: a whole 4x4x4 slice. The times are simulated.
128 devices in a mesh: grp: 2 (over core), pts: 64 (over x, z, y).
Axes of the slice: x: 4, y: 4, z: 4, core: 2. Of those that a mesh axis runs over, the one named last changes fastest.
Arguments:
- points_z: bfloat16 [131072, 256], P(('grp', 'pts')), may hold values from -40 to 40
- patch_len: int32 [128], P(('grp', 'pts')), may hold values from 961 to 1024
- z_dest: int32 [1024], P(('grp', 'pts')), may hold values from 0 to 1023, as said below
- cell_of: int32 [131072], P(('grp', 'pts')), may hold values from 0 to 32767, as said below
- norm_gain: float32 [2, 2, 256], replicated, may hold values from 0.25 to 1.75
- qkv_weight: bfloat16 [2, 256, 768], replicated, may hold values from -8 to 8
- out_weight: bfloat16 [2, 256, 256], replicated, may hold values from -0.375 to 0.375
- up_weight: bfloat16 [2, 256, 1024], replicated, may hold values from -0.375 to 0.375
- down_weight: bfloat16 [2, 1024, 256], replicated, may hold values from -0.1875 to 0.1875
- pool_weight: bfloat16 [256, 512], replicated, may hold values from -0.375 to 0.375
Outputs:
- pooled: bfloat16 [32768, 512], P(('grp', 'pts'))
Inputs may be any that keep to these rules, and one draw needn't show every extreme that they name: z_dest is a permutation of the block numbers. With devices taken in the order grp then pts, cyclically, and D their number, a block of the device of index i goes to the device of index i + delta, where the set of deltas is the same on every device: every value from -4 + 1 to 3, and D / 2; each delta is taken by exactly 1 block of a device. cell_of never falls along the points in the order grp then pts. Each device starts exactly 256 cells, numbered from its index times 256; its points before its first start belong to the last cell of the previous device; the first point of all starts cell 0.
All inputs are finite; a program needn't handle non-finite values.
Results may differ from a plain program's by a relative error of at most 0.012.
Values may be sent and summed in bfloat16 or wider, within the bound.
A program may use at most 64 MiB of HBM per device.

v0:
```python
import jax
import jax.numpy as jnp
from jax import lax
from jax.sharding import PartitionSpec as P

C = 256
HEADS = 16
PATCH = 1024
BLK = 128
REACH = 4
CELL_DEV = 256


NORM_EPS = 1e-05


def passed_along(block, axis, distance):
    devices = range(lax.axis_size(axis))
    route = [(i - distance, i) for i in devices if i - distance in devices]
    return lax.ppermute(block, axis, route)


def stored(values):
    return lax.optimization_barrier(values.astype(jnp.bfloat16))


def normalize(features, gain_row):
    widened = features.astype(jnp.float32)
    centered = widened - jnp.mean(widened, axis=-1, keepdims=True)
    variance = jnp.mean(centered * centered, axis=-1, keepdims=True)
    return (centered * lax.rsqrt(variance + NORM_EPS) * gain_row).astype(jnp.bfloat16)


def patch_attention(projected, key_live):
    row_count = projected.shape[0]
    patches = row_count // PATCH
    head_size = C // HEADS
    per_step = 2
    step_count = HEADS // per_step
    step_width = per_step * head_size
    scaling = head_size ** (-0.5)

    def split_heads(columns):
        return (
            columns.reshape(patches, PATCH, step_count, step_width)
            .transpose(0, 2, 1, 3)
            .reshape(patches * step_count, PATCH, step_width)
        )

    queries = split_heads(projected[:, :C])
    keys_all = split_heads(projected[:, C : 2 * C])
    values = split_heads(projected[:, 2 * C :])
    live_keys = jnp.repeat(key_live.reshape(patches, 1, PATCH), step_count, axis=1).reshape(
        patches * step_count, PATCH
    )

    def one_step(entries):
        query_rows = entries[0].reshape(PATCH, per_step, head_size)
        key_rows = entries[1].reshape(PATCH, per_step, head_size)
        value_rows = entries[2].reshape(PATCH, per_step, head_size)
        scores = (
            jnp.einsum("qhd,khd->hqk", query_rows, key_rows, preferred_element_type=jnp.float32)
            * scaling
        )
        scores = jnp.where(entries[3][None, None, :], scores, -jnp.inf)
        row_max = jnp.max(scores, axis=-1, keepdims=True)
        weights = jnp.exp(scores - row_max)
        denominator = jnp.sum(weights, axis=-1)
        attended = jnp.einsum(
            "hqk,khd->qhd", stored(weights), value_rows, preferred_element_type=jnp.float32
        )
        return stored(attended / denominator.T[:, :, None]).reshape(PATCH, step_width)

    results = lax.map(one_step, (queries, keys_all, values, live_keys))
    return (
        results.reshape(patches, step_count, PATCH, step_width)
        .transpose(0, 2, 1, 3)
        .reshape(row_count, C)
    )


def transformer_block(
    points, key_live, gain_pair, qkv_weights, out_weights, up_weights, down_weights
):
    normed = normalize(points, gain_pair[0])
    projected = stored(jnp.dot(normed, qkv_weights, preferred_element_type=jnp.float32))
    attended = patch_attention(projected, key_live)
    residual = stored(
        points.astype(jnp.float32)
        + jnp.dot(attended, out_weights, preferred_element_type=jnp.float32)
    )
    hidden = stored(
        jax.nn.gelu(
            jnp.dot(
                normalize(residual, gain_pair[1]), up_weights, preferred_element_type=jnp.float32
            ),
            approximate=False,
        )
    )
    return stored(
        residual.astype(jnp.float32)
        + jnp.dot(hidden, down_weights, preferred_element_type=jnp.float32)
    )


def on_device(
    points_z,
    patch_len,
    z_dest,
    cell_of,
    norm_gain,
    qkv_weight,
    out_weight,
    up_weight,
    down_weight,
    pool_weight,
):
    point_count, channels = points_z.shape
    block_count = z_dest.shape[0]
    devices = lax.axis_size(("grp", "pts"))
    device_index = lax.axis_index(("grp", "pts"))
    position = jnp.arange(point_count) % PATCH
    keep_z = position < jnp.repeat(patch_len, PATCH)
    first = transformer_block(
        points_z, keep_z, norm_gain[0], qkv_weight[0], out_weight[0], up_weight[0], down_weight[0]
    )
    blocks = jnp.concatenate(
        [first.reshape(block_count, BLK, channels), jnp.zeros((1, BLK, channels), jnp.bfloat16)]
    )
    block_keep = jnp.concatenate(
        [keep_z.astype(jnp.bfloat16).reshape(block_count, BLK), jnp.zeros((1, BLK), jnp.bfloat16)]
    )
    target = z_dest // block_count
    target_slot = z_dest % block_count
    slot_code = jnp.concatenate([target_slot, jnp.full((1,), -1, jnp.int32)]).astype(jnp.bfloat16)
    numbers = jnp.arange(block_count)
    same_target = target[:, None] == target[None, :]
    earlier = numbers[None, :] < numbers[:, None]
    rank_within = jnp.sum(same_target & earlier, axis=1)
    per_pair = block_count // (2 * REACH)
    placed_at = target * per_pair + rank_within
    send_order = jnp.full((devices * per_pair,), block_count, jnp.int32).at[placed_at].set(numbers)
    sent_rows = blocks[send_order]
    sent_keep = block_keep[send_order]
    sent_slot = slot_code[send_order][:, None]
    arrived_rows, arrived_keep, arrived_slot = (
        lax.all_to_all(sent_rows, ("grp", "pts"), split_axis=0, concat_axis=0, tiled=True),
        lax.all_to_all(sent_keep, ("grp", "pts"), split_axis=0, concat_axis=0, tiled=True),
        lax.all_to_all(sent_slot, ("grp", "pts"), split_axis=0, concat_axis=0, tiled=True),
    )
    incoming = arrived_slot[:, 0].astype(jnp.int32)
    wanted = incoming[None, :] == numbers[:, None]
    source = jnp.sum(jnp.where(wanted, jnp.arange(incoming.shape[0])[None, :], 0), axis=1)
    regrouped = arrived_rows[source].reshape(point_count, channels)
    keep_h = arrived_keep[source].reshape(point_count) > 0.5
    second = transformer_block(
        regrouped, keep_h, norm_gain[1], qkv_weight[1], out_weight[1], up_weight[1], down_weight[1]
    )
    cell_slot = cell_of - device_index * CELL_DEV
    rim_row = ((cell_slot == -1) & keep_h).astype(jnp.bfloat16)[None, :]
    rim_sum = jnp.dot(rim_row, second, preferred_element_type=jnp.float32)
    rim_count = jnp.sum(rim_row.astype(jnp.float32), axis=1)
    next_sum, next_count = passed_along((rim_sum, rim_count), ("grp", "pts"), -1)
    member_table = ((cell_slot[None, :] == jnp.arange(CELL_DEV)[:, None]) & keep_h[None, :]).astype(
        jnp.bfloat16
    )
    cell_sums = jnp.dot(member_table, second, preferred_element_type=jnp.float32)
    counts = jnp.sum(member_table.astype(jnp.float32), axis=1)
    cell_sums = cell_sums.at[CELL_DEV - 1].add(next_sum[0])
    counts = counts.at[CELL_DEV - 1].add(next_count[0])
    mean_rows = stored(cell_sums / jnp.maximum(counts, 1.0)[:, None])
    return stored(
        jax.nn.gelu(
            jnp.dot(mean_rows, pool_weight, preferred_element_type=jnp.float32), approximate=False
        )
    )


def solution(mesh):
    placed = (
        P(("grp", "pts"), None),
        P(("grp", "pts")),
        P(("grp", "pts")),
        P(("grp", "pts")),
        P(),
        P(),
        P(),
        P(),
        P(),
        P(),
    )
    return jax.shard_map(
        on_device, mesh=mesh, in_specs=placed, out_specs=P(("grp", "pts"), None), check_vma=False
    )
```

profile of v0, /device:TPU:24, one launch (start us, length us, event | category | flops | bytes accessed | tf_op | source)
XLA Modules:
  0.0 337.7 jit_solution(14689891488846518718)
XLA Ops:
  2.2 4.9 %fusion.113 = bf16[128,1,1]{0,2,1:T(2,128)(2,1)S(1)} fusion(bf16[]{:T(256)} %bitcast.14, bf16[]{:T(256)} %bitcast.15, bf16[]{:T(256)} %bitcast.16, bf16[]{:T(256)} %bitcast.17, bf16[]{:T(256)} %bitcast.18, bf16[]{:T(256)} %bitcast.19, bf16[]{:T(256)} %bitcast.20, bf16[]{:T(256)} %bitcast.21, s32[128]{0:T(128)S(1)} %scatter_custom_fusion), kind=kLoop, calls=%fused_computation.216 | loop fusion | flops 2432 | bytes 784 | tf_op jit(solution)/shard_map/all_to_all | solution.py:149
  7.9 10.3 %all-to-all-start.1 = ((bf16[128,1,1]{2,1,0:T(2,128)(2,1)}), bf16[128,1,1]{2,1,0:T(2,128)(2,1)S(1)}, u32[]{:S(2)}, u32[]{:S(2)}) async-start(bf16[128,1,1]{2,1,0:T(2,128)(2,1)} %copy.50), calls=%async_computation.1 | async-start | bytes 131072 | tf_op jit(solution)/shard_map/all_to_all | solution.py:149
  25.1 61.4 %while.22 = (s32[]{:T(128)}, bf16[8,1024,32]{1,2,0:T(8,128)(2,1)S(1)}, bf16[8,1024,32]{1,2,0:T(8,128)(2,1)S(1)}, pred[8,1024]{1,0:T(8,128)(4,1)S(1)}, bf16[8,102...) while((s32[]{:T(128)}, bf16[8,1024,32]{1,2,0:T(8,128)(2,1)S(1)}, ...), condition=%wide.region_8.9_spmd, body=%wide.region_5.8_spmd.sunk | while | flops 144770048 | bytes 9194589 | solution.py:74
  25.1 4.7 %fusion.162 = (f32[2,1024]{1,0:T(2,128)S(1)}, bf16[2,1024,1024]{1,2,0:T(8,128)(2,1)}) fusion(pred[1024]{0:T(1024)(128)(4,1)S(1)} %dynamic-slice_reduce_fusion.4, bf16[1024,2,16]{0,2,1:T(8,128)(2,1)S(1)} %bitcast.191, bf16[1024,2,16]{0,2,1:T(8,128)(2,1)S(1)} %bitcast.190), kind=kOutput, calls=%fused_computation.222.clone.1 | convolution fusion | flops 77595648 | bytes 4334592 | tf_op jit(solution)/shard_map/while/body/eval_jaxpr/sub | solution.py:67
  32.8 4.7 %fusion.162 = (f32[2,1024]{1,0:T(2,128)S(1)}, bf16[2,1024,1024]{1,2,0:T(8,128)(2,1)}) fusion(pred[1024]{0:T(1024)(128)(4,1)S(1)} %dynamic-slice_reduce_fusion.4, bf16[1024,2,16]{0,2,1:T(8,128)(2,1)S(1)} %bitcast.191, bf16[1024,2,16]{0,2,1:T(8,128)(2,1)S(1)} %bitcast.190), kind=kOutput, calls=%fused_computation.222.clone.1 | convolution fusion | flops 77595648 | bytes 4334592 | tf_op jit(solution)/shard_map/while/body/eval_jaxpr/sub | solution.py:67
  40.5 4.7 %fusion.162 = (f32[2,1024]{1,0:T(2,128)S(1)}, bf16[2,1024,1024]{1,2,0:T(8,128)(2,1)}) fusion(pred[1024]{0:T(1024)(128)(4,1)S(1)} %dynamic-slice_reduce_fusion.4, bf16[1024,2,16]{0,2,1:T(8,128)(2,1)S(1)} %bitcast.191, bf16[1024,2,16]{0,2,1:T(8,128)(2,1)S(1)} %bitcast.190), kind=kOutput, calls=%fused_computation.222.clone.1 | convolution fusion | flops 77595648 | bytes 4334592 | tf_op jit(solution)/shard_map/while/body/eval_jaxpr/sub | solution.py:67
  48.1 4.7 %fusion.162 = (f32[2,1024]{1,0:T(2,128)S(1)}, bf16[2,1024,1024]{1,2,0:T(8,128)(2,1)}) fusion(pred[1024]{0:T(1024)(128)(4,1)S(1)} %dynamic-slice_reduce_fusion.4, bf16[1024,2,16]{0,2,1:T(8,128)(2,1)S(1)} %bitcast.191, bf16[1024,2,16]{0,2,1:T(8,128)(2,1)S(1)} %bitcast.190), kind=kOutput, calls=%fused_computation.222.clone.1 | convolution fusion | flops 77595648 | bytes 4334592 | tf_op jit(solution)/shard_map/while/body/eval_jaxpr/sub | solution.py:67
  55.8 4.7 %fusion.162 = (f32[2,1024]{1,0:T(2,128)S(1)}, bf16[2,1024,1024]{1,2,0:T(8,128)(2,1)}) fusion(pred[1024]{0:T(1024)(128)(4,1)S(1)} %dynamic-slice_reduce_fusion.4, bf16[1024,2,16]{0,2,1:T(8,128)(2,1)S(1)} %bitcast.191, bf16[1024,2,16]{0,2,1:T(8,128)(2,1)S(1)} %bitcast.190), kind=kOutput, calls=%fused_computation.222.clone.1 | convolution fusion | flops 77595648 | bytes 4334592 | tf_op jit(solution)/shard_map/while/body/eval_jaxpr/sub | solution.py:67
  63.5 4.7 %fusion.162 = (f32[2,1024]{1,0:T(2,128)S(1)}, bf16[2,1024,1024]{1,2,0:T(8,128)(2,1)}) fusion(pred[1024]{0:T(1024)(128)(4,1)S(1)} %dynamic-slice_reduce_fusion.4, bf16[1024,2,16]{0,2,1:T(8,128)(2,1)S(1)} %bitcast.191, bf16[1024,2,16]{0,2,1:T(8,128)(2,1)S(1)} %bitcast.190), kind=kOutput, calls=%fused_computation.222.clone.1 | convolution fusion | flops 77595648 | bytes 4334592 | tf_op jit(solution)/shard_map/while/body/eval_jaxpr/sub | solution.py:67
  71.2 4.7 %fusion.162 = (f32[2,1024]{1,0:T(2,128)S(1)}, bf16[2,1024,1024]{1,2,0:T(8,128)(2,1)}) fusion(pred[1024]{0:T(1024)(128)(4,1)S(1)} %dynamic-slice_reduce_fusion.4, bf16[1024,2,16]{0,2,1:T(8,128)(2,1)S(1)} %bitcast.191, bf16[1024,2,16]{0,2,1:T(8,128)(2,1)S(1)} %bitcast.190), kind=kOutput, calls=%fused_computation.222.clone.1 | convolution fusion | flops 77595648 | bytes 4334592 | tf_op jit(solution)/shard_map/while/body/eval_jaxpr/sub | solution.py:67
  78.8 4.7 %fusion.162 = (f32[2,1024]{1,0:T(2,128)S(1)}, bf16[2,1024,1024]{1,2,0:T(8,128)(2,1)}) fusion(pred[1024]{0:T(1024)(128)(4,1)S(1)} %dynamic-slice_reduce_fusion.4, bf16[1024,2,16]{0,2,1:T(8,128)(2,1)S(1)} %bitcast.191, bf16[1024,2,16]{0,2,1:T(8,128)(2,1)S(1)} %bitcast.190), kind=kOutput, calls=%fused_computation.222.clone.1 | convolution fusion | flops 77595648 | bytes 4334592 | tf_op jit(solution)/shard_map/while/body/eval_jaxpr/sub | solution.py:67
  87.5 12.0 %fusion.24 = bf16[1024,1024]{1,0:T(8,128)(2,1)} fusion(bf16[1024,256]{1,0:T(8,128)(2,1)S(1)} %fusion.42, bf16[2,256,1024]{2,1,0:T(8,128)(2,1)} %param.25, f32[256]{0:T(256)S(1)} %bitcast.207, f32[1024]{0:T(1024)S(1)} %add_rsqrt_fusion.2, f32[1024]{0:T(1024)S(1)} %broadcast_multiply_fusion.2), kind=kOutput, calls=%fused_computation.45 | convolution fusion | flops 606339072 | bytes 3154944 | tf_op jit(solution)/shard_map/dot_general | solution.py:94
  100.9 9.8 %all-to-all-start = ((bf16[128,1,128]{2,1,0:T(2,128)(2,1)}), bf16[128,1,128]{2,1,0:T(2,128)(2,1)S(1)}, u32[]{:S(2)}, u32[]{:S(2)}) async-start(bf16[128,1,128]{2,1,0:T(2,128)(2,1)} %copy.49), calls=%async_computation | async-start | bytes 131072 | tf_op jit(solution)/shard_map/all_to_all | solution.py:148
  113.0 6.3 %gather_fusion.2 = bf16[128,128,256]{2,1,0:T(8,128)(2,1)} fusion(bf16[9,128,256]{2,1,0:T(8,128)(2,1)S(1)} %concatenate.19, s32[1024]{0:T(1024)S(1)} %pad_clamp_fusion.1), kind=kCustom, calls=%fused_computation.2 | custom fusion | bytes 16777728 | tf_op jit(solution)/shard_map/gather | solution.py:143
  119.3 10.2 %all-to-all-start.2 = ((bf16[128,128,256]{2,1,0:T(8,128)(2,1)}), bf16[128,128,256]{2,1,0:T(8,128)(2,1)}, u32[]{:S(2)}, u32[]{:S(2)}) async-start(bf16[128,128,256]{2,1,0:T(8,128)(2,1)} %gather_fusion.2), calls=%async_computation.2 | async-start | bytes 16777216 | tf_op jit(solution)/shard_map/all_to_all | solution.py:147
  136.2 99.6 %collective-permute-done.1 = f32[1]{0:T(128)} collective-permute-done((f32[1]{0:T(128)}, f32[1]{0:T(128)}, u32[]{:S(2)}, u32[]{:S(2)}) %collective-permute-start.1) | collective-permute-done | bytes 36 | tf_op jit(solution)/shard_map/ppermute | solution.py:20
  236.6 10.7 %all-to-all-done.2 = bf16[128,128,256]{2,1,0:T(8,128)(2,1)} async-done(((bf16[128,128,256]{2,1,0:T(8,128)(2,1)}), bf16[128,128,256]{2,1,0:T(8,128)(2,1)}, u32[]{:S(2)}, u32[]{:S(2)}) %all-to-all-start.2) | async-done | bytes 8388640 | tf_op jit(solution)/shard_map/all_to_all | solution.py:147
  253.6 61.4 %while.23 = (s32[]{:T(128)}, bf16[8,1024,32]{1,2,0:T(8,128)(2,1)S(1)}, bf16[8,1024,32]{1,2,0:T(8,128)(2,1)S(1)}, pred[8,1024]{1,0:T(8,128)(4,1)S(1)}, bf16[8,102...) while((s32[]{:T(128)}, bf16[8,1024,32]{1,2,0:T(8,128)(2,1)S(1)}, ...), condition=%wide.region_16.17_spmd, body=%wide.region_13.16_spmd.sunk | while | flops 144770048 | bytes 9194589 | solution.py:74
  253.7 4.7 %fusion.168 = (f32[2,1024]{1,0:T(2,128)S(1)}, bf16[2,1024,1024]{1,2,0:T(8,128)(2,1)}) fusion(pred[1024]{0:T(1024)(128)(4,1)S(1)} %dynamic-slice_reduce_fusion.5, bf16[1024,2,16]{0,2,1:T(8,128)(2,1)S(1)} %bitcast.193, bf16[1024,2,16]{0,2,1:T(8,128)(2,1)S(1)} %bitcast.192), kind=kOutput, calls=%fused_computation.223.clone.1 | convolution fusion | flops 77595648 | bytes 4334592 | tf_op jit(solution)/shard_map/while/body/eval_jaxpr/sub | solution.py:67
  292.0 4.7 %fusion.168 = (f32[2,1024]{1,0:T(2,128)S(1)}, bf16[2,1024,1024]{1,2,0:T(8,128)(2,1)}) fusion(pred[1024]{0:T(1024)(128)(4,1)S(1)} %dynamic-slice_reduce_fusion.5, bf16[1024,2,16]{0,2,1:T(8,128)(2,1)S(1)} %bitcast.193, bf16[1024,2,16]{0,2,1:T(8,128)(2,1)S(1)} %bitcast.192), kind=kOutput, calls=%fused_computation.223.clone.1 | convolution fusion | flops 77595648 | bytes 4334592 | tf_op jit(solution)/shard_map/while/body/eval_jaxpr/sub | solution.py:67
  299.7 4.7 %fusion.168 = (f32[2,1024]{1,0:T(2,128)S(1)}, bf16[2,1024,1024]{1,2,0:T(8,128)(2,1)}) fusion(pred[1024]{0:T(1024)(128)(4,1)S(1)} %dynamic-slice_reduce_fusion.5, bf16[1024,2,16]{0,2,1:T(8,128)(2,1)S(1)} %bitcast.193, bf16[1024,2,16]{0,2,1:T(8,128)(2,1)S(1)} %bitcast.192), kind=kOutput, calls=%fused_computation.223.clone.1 | convolution fusion | flops 77595648 | bytes 4334592 | tf_op jit(solution)/shard_map/while/body/eval_jaxpr/sub | solution.py:67
  307.4 4.7 %fusion.168 = (f32[2,1024]{1,0:T(2,128)S(1)}, bf16[2,1024,1024]{1,2,0:T(8,128)(2,1)}) fusion(pred[1024]{0:T(1024)(128)(4,1)S(1)} %dynamic-slice_reduce_fusion.5, bf16[1024,2,16]{0,2,1:T(8,128)(2,1)S(1)} %bitcast.193, bf16[1024,2,16]{0,2,1:T(8,128)(2,1)S(1)} %bitcast.192), kind=kOutput, calls=%fused_computation.223.clone.1 | convolution fusion | flops 77595648 | bytes 4334592 | tf_op jit(solution)/shard_map/while/body/eval_jaxpr/sub | solution.py:67
  316.0 11.2 %fusion.27 = bf16[1024,1024]{1,0:T(8,128)(2,1)S(1)} fusion(bf16[1024,256]{1,0:T(8,128)(2,1)S(1)} %fusion.45, bf16[2,256,1024]{2,1,0:T(8,128)(2,1)} %param.25, f32[256]{0:T(256)S(1)} %bitcast.206, f32[1024]{0:T(1024)S(1)} %add_rsqrt_fusion, f32[1024]{0:T(1024)S(1)} %broadcast_multiply_fusion.1), kind=kOutput, calls=%fused_computation.48 | convolution fusion | flops 606339072 | bytes 3154944 | tf_op jit(solution)/shard_map/dot_general | solution.py:94
  330.8 4.8 %collective-permute-done = f32[1,256]{1,0:T(1,128)S(1)} collective-permute-done((f32[1,256]{1,0:T(1,128)S(1)}, f32[1,256]{1,0:T(1,128)S(1)}, u32[]{:S(2)}, u32[]{:S(2)}) %collective-permute-start) | collective-permute-done | bytes 1056 | tf_op jit(solution)/shard_map/ppermute | solution.py:20
  (171 shorter events, 99.6 us)
Async XLA Ops:
  0.0 335.8 %copy-start = (bf16[256,512]{1,0:T(8,128)(2,1)S(1)}, bf16[256,512]{1,0:T(8,128)(2,1)}, u32[]{:S(2)}) copy-start(bf16[256,512]{1,0:T(8,128)(2,1)} %param.27) | copy-start | bytes 786436
  7.9 93.0 %all-to-all-start.1 = ((bf16[128,1,1]{2,1,0:T(2,128)(2,1)}), bf16[128,1,1]{2,1,0:T(2,128)(2,1)S(1)}, u32[]{:S(2)}, u32[]{:S(2)}) async-start(bf16[128,1,1]{2,1,0:T(2,128)(2,1)} %copy.50), calls=%async_computation.1 | async-start | bytes 131072 | tf_op jit(solution)/shard_map/all_to_all | solution.py:149
  25.0 61.4 %copy-start.1 = (bf16[1024,256]{1,0:T(8,128)(2,1)S(1)}, bf16[1024,256]{1,0:T(8,128)(2,1)}, u32[]{:S(2)}) copy-start(bf16[1024,256]{1,0:T(8,128)(2,1)} %param.18) | copy-start | bytes 1572868
  25.1 61.4 %copy-start.2 = (bf16[2,256,256]{2,1,0:T(8,128)(2,1)S(1)}, bf16[2,256,256]{2,1,0:T(8,128)(2,1)}, u32[]{:S(2)}) copy-start(bf16[2,256,256]{2,1,0:T(8,128)(2,1)} %param.24) | copy-start | bytes 786436
  87.5 23.2 %copy-start.5 = (bf16[2,1024,256]{2,1,0:T(8,128)(2,1)S(1)}, bf16[2,1024,256]{2,1,0:T(8,128)(2,1)}, u32[]{:S(2)}) copy-start(bf16[2,1024,256]{2,1,0:T(8,128)(2,1)} %param.26) | copy-start | bytes 3145732
  100.9 18.4 %all-to-all-start = ((bf16[128,1,128]{2,1,0:T(2,128)(2,1)}), bf16[128,1,128]{2,1,0:T(2,128)(2,1)S(1)}, u32[]{:S(2)}, u32[]{:S(2)}) async-start(bf16[128,1,128]{2,1,0:T(2,128)(2,1)} %copy.49), calls=%async_computation | async-start | bytes 131072 | tf_op jit(solution)/shard_map/all_to_all | solution.py:148
  119.3 13.3 %copy-start.4 = (s32[1024]{0:T(1024)S(1)}, s32[1024]{0:T(1024)}, u32[]{:S(2)}) copy-start(s32[1024]{0:T(1024)} %param.21) | copy-start | bytes 12292
  119.3 132.9 %copy-start.3 = (bf16[2,256,768]{2,1,0:T(8,128)(2,1)S(1)}, bf16[2,256,768]{2,1,0:T(8,128)(2,1)}, u32[]{:S(2)}) copy-start(bf16[2,256,768]{2,1,0:T(8,128)(2,1)} %param.23) | copy-start | bytes 2359300
  119.3 128.0 %all-to-all-start.2 = ((bf16[128,128,256]{2,1,0:T(8,128)(2,1)}), bf16[128,128,256]{2,1,0:T(8,128)(2,1)}, u32[]{:S(2)}, u32[]{:S(2)}) async-start(bf16[128,128,256]{2,1,0:T(8,128)(2,1)} %gather_fusion.2), calls=%async_computation.2 | async-start | bytes 16777216 | tf_op jit(solution)/shard_map/all_to_all | solution.py:147
  133.2 102.5 %collective-permute-start.1 = (f32[1]{0:T(128)}, f32[1]{0:T(128)}, u32[]{:S(2)}, u32[]{:S(2)}) collective-permute-start(f32[1]{0:T(128)} %bitcast.66), channel_id=1, source_target_pairs={{1,0},{2,1},{3,2},{4,3},{5,4},{6,5},{7,6},{8,7},{9,8},{10,9},{11,1... | collective-permute-start | bytes 20 | tf_op jit(solution)/shard_map/ppermute | solution.py:20
  316.0 11.2 %copy-start.6 = (bf16[2,1024,256]{2,1,0:T(8,128)(2,1)S(1)}, bf16[2,1024,256]{2,1,0:T(8,128)(2,1)}, u32[]{:S(2)}) copy-start(bf16[2,1024,256]{2,1,0:T(8,128)(2,1)} %param.26) | copy-start | bytes 3145732
  328.0 7.6 %collective-permute-start = (f32[1,256]{1,0:T(1,128)S(1)}, f32[1,256]{1,0:T(1,128)S(1)}, u32[]{:S(2)}, u32[]{:S(2)}) collective-permute-start(f32[1,256]{1,0:T(1,128)S(1)} %fusion.123), channel_id=1, source_target_pairs={{1,0},{2,1},{3,2},{4,3},{5,4},{6,5},{7,6},{8,7},{9,8},{10,9},{11,1... | collective-permute-start | bytes 3080 | tf_op jit(solution)/shard_map/ppermute | solution.py:20
where the time goes:
time: 339 us; the launch traced here: 338 us
  matrix products  153 us (45%)
  waiting for transfers between devices  115 us (34%)
  starting transfers between devices  35.4 us (10%)
  local copies, waits for them, and re-layouts  17.7 us (5%)
  other arithmetic  14.9 us (4%)
    ppermute x2, waiting for transfers between devices, passed_along(): return lax.ppermute(block, axis, route)  104 us
    sub x16, matrix products, one_step(): weights = jnp.exp(scores - row_max)  75.7 us
    dot_general x16, matrix products, one_step(): jnp.einsum('hqk,khd->qhd', stored(weights), value_rows, preferred_element...  45.5 us
    dot_general x2, matrix products, transformer_block(): jnp.dot(normalize(residual, gain_pair[1]), up_weights, preferred_element_...  23.1 us
    all_to_all x1, waiting for transfers between devices, on_device(): lax.all_to_all(sent_rows, ('grp', 'pts'), split_axis=0, concat_axis=0, ti...  10.7 us
    all_to_all x1, starting transfers between devices, on_device(): lax.all_to_all(sent_slot, ('grp', 'pts'), split_axis=0, concat_axis=0, ti...  10.3 us
    all_to_all x1, starting transfers between devices, on_device(): lax.all_to_all(sent_rows, ('grp', 'pts'), split_axis=0, concat_axis=0, ti...  10.2 us
    all_to_all x1, starting transfers between devices, on_device(): lax.all_to_all(sent_keep, ('grp', 'pts'), split_axis=0, concat_axis=0, ti...  9.76 us
  transfers between devices with their start and end apart: 5, of which 3 were waited for; matrix products, arithmetic and copies ran while one was open for 28% of the time, Pallas kernels for 0%

commit v1 on v0

v1 whole, which is shorter than its diff:
```python
import functools

import jax
import jax.numpy as jnp
from jax import lax
from jax.experimental import pallas as pl
from jax.experimental.pallas import tpu as pltpu
from jax.sharding import PartitionSpec as P

C = 256
HEADS = 16
HD = 16
PATCH = 1024
BLK = 128
NB = 8
CELL_DEV = 256
CP = 512
FF = 1024
NORM_EPS = 1e-05
QW = 512
ROWS = 256
LOG2E = 1.4426950408889634
POOL_ROWS = 272
ERF = (
    0.7978722361090334,
    0.03636660609986694,
    -5.8514434084682766e-05,
    -4.7090980998381986e-05,
    2.779316469575001e-06,
    -5.589976858483281e-08,
)
ERF_END = 5.6 * 5.6
bf16 = jnp.bfloat16
f32 = jnp.float32
MESH = pl.DeviceIdType.MESH


def gelu(x):
    u = jnp.minimum(x * x, ERF_END)
    r = ERF[5]
    for coefficient in ERF[4::-1]:
        r = r * u + coefficient
    half = 0.5 * x
    return half + half * jnp.tanh(x * r)


def norm(x, gain):
    centered = x - jnp.mean(x, axis=-1, keepdims=True)
    variance = jnp.mean(centered * centered, axis=-1, keepdims=True)
    return (centered * lax.rsqrt(variance + NORM_EPS) * gain).astype(bf16)


def dot(a, b):
    return jnp.dot(a, b, preferred_element_type=f32)


def dot_nt(a, b):
    return lax.dot_general(a, b, (((1,), (1,)), ((), ())), preferred_element_type=f32)


def dot_tn(a, b):
    return lax.dot_general(a, b, (((0,), (0,)), ((), ())), preferred_element_type=f32)


def project(b, chunk, xs, meta, gain, wqkv, wqv_t, kk, qt, vt):
    rows = pl.ds(chunk * ROWS, ROWS)
    xn = norm(xs[rows, :].astype(f32), gain[b, 0:1, :])
    k = dot(xn, wqkv[b, :, C : 2 * C])
    for part in range(2):
        slot = chunk * 2 + part
        limit = meta[slot, 1:2, :]
        live = lax.broadcasted_iota(jnp.int32, (BLK, C), 0) < limit
        piece = k[part * BLK : (part + 1) * BLK, :]
        piece = jnp.where(live, piece, piece[0:1, :]).astype(bf16)
        at = pl.ds(slot * BLK, BLK)
        for g in range(2):
            lanes = piece[:, g * 128 : (g + 1) * 128]
            kk[g, at, 0:128] = lanes
            kk[g, at, 128:256] = lanes
    qv = dot_nt(wqv_t[...], xn)
    q = qv[:C, :].astype(bf16).astype(f32) * (HD**-0.5 * LOG2E)
    hi = q.astype(bf16)
    lo = (q - hi.astype(f32)).astype(bf16)
    for h in range(HEADS):
        r = (h % 8) * HD
        qt[h, r : r + HD, rows] = hi[h * HD : (h + 1) * HD, :]
        qt[h, 128 + r : 128 + r + HD, rows] = lo[h * HD : (h + 1) * HD, :]
    limits = jnp.concatenate(
        [meta[chunk * 2, 1:2, 0:BLK], meta[chunk * 2 + 1, 1:2, 0:BLK]], axis=1
    )
    lane = lax.broadcasted_iota(jnp.int32, (1, ROWS), 1) % BLK
    live_row = (lane < limits).astype(f32)
    v = (qv[C:, :] * live_row).astype(bf16)
    first = lax.broadcasted_iota(jnp.int32, (HD, ROWS), 0) == 0
    ones = jnp.where(first, live_row, 0.0).astype(bf16)
    for h in range(HEADS):
        vt[h, 0:HD, rows] = v[h * HD : (h + 1) * HD, :]
        vt[h, HD : 2 * HD, rows] = ones


def attention(kk, qt, vt, ot, s_a, s_b, m_a, m_b):
    tiles = PATCH // QW

    def scores(h, t, s, m):
        raw = dot(kk[h // 8], qt[h, :, pl.ds(t * QW, QW)])
        s[...] = raw
        m[...] = jnp.max(raw.reshape(PATCH // 8, 8, QW), axis=0)

    def values(h, t, s, m):
        top = jnp.max(m[...], axis=0, keepdims=True)
        total = None
        for c in range(PATCH // 256):
            keys = pl.ds(c * 256, 256)
            e = jnp.exp2(s[keys, :] - top).astype(bf16)
            part = dot(vt[h, :, keys], e)
            total = part if total is None else total + part
        ot[pl.ds(pl.multiple_of(h * HD, HD), HD), pl.ds(t * QW, QW)] = (
            total[0:HD, :] / total[HD : HD + 1, :]
        ).astype(bf16)

    scores(0, 0, s_a, m_a)

    def head(h, carry):
        for t in range(tiles):
            now = (s_a, m_a) if t % 2 == 0 else (s_b, m_b)
            later = (s_b, m_b) if t % 2 == 0 else (s_a, m_a)
            next_h = h if t < tiles - 1 else jnp.minimum(h + 1, HEADS - 1)
            scores(next_h, (t + 1) % tiles, *later)
            values(h, t, *now)
        return carry

    lax.fori_loop(0, HEADS, head, 0)


def finish(b, chunk, xs, gain, ot, wo, wup, wdown):
    rows = pl.ds(chunk * ROWS, ROWS)
    h = xs[rows, :].astype(f32) + dot_tn(ot[:, rows], wo[b])
    h = h.astype(bf16).astype(f32)
    hn = norm(h, gain[b, 1:2, :])
    u = gelu(dot(hn, wup[b])).astype(bf16)
    return (h + dot(u, wdown[b])).astype(bf16)


def transpose_weights(b, wqkv, wqv_t):
    for part, first in enumerate((0, 2 * C)):
        w = wqkv[b, :, first : first + C].astype(f32)
        wqv_t[part * C : (part + 1) * C, :] = w.T.astype(bf16)


def body(
    deltas,
    devices,
    n_pts,
    patch_len,
    z_dest,
    x_ref,
    cells,
    gain,
    wqkv,
    wo,
    wup,
    wdown,
    wpool,
    out,
    x_first,
    x_second,
    y_send,
    wqv_t,
    kk,
    qt,
    vt,
    ot,
    s_a,
    s_b,
    m_a,
    m_b,
    meta_send,
    meta_recv,
    rim_send,
    rim_recv,
    send_sem,
    recv_sem,
    meta_send_sem,
    meta_recv_sem,
    rim_send_sem,
    rim_recv_sem,
):
    me = lax.axis_index("grp") * n_pts + lax.axis_index("pts")

    def device(delta):
        flat = (me + delta + devices) % devices
        return (flat // n_pts, flat % n_pts)

    barrier = pltpu.get_barrier_semaphore()
    for delta in deltas:
        if delta:
            pl.semaphore_signal(barrier, inc=1, device_id=device(delta), device_id_type=MESH)
    pl.semaphore_wait(barrier, NB - 1)

    def remote(src, dst, ssem, rsem, delta):
        return pltpu.make_async_remote_copy(
            src_ref=src, dst_ref=dst, send_sem=ssem, recv_sem=rsem,
            device_id=device(delta), device_id_type=MESH,
        )

    def block_copy(slot):
        rows = pl.ds(slot * BLK, BLK)
        return remote(
            y_send.at[rows], x_second.at[rows], send_sem.at[slot], recv_sem.at[slot], deltas[slot]
        )

    def meta_copy(slot):
        return remote(
            meta_send.at[slot], meta_recv.at[slot], meta_send_sem.at[slot],
            meta_recv_sem.at[slot], deltas[slot],
        )

    row = lax.broadcasted_iota(jnp.int32, (8, C), 0)
    for slot, delta in enumerate(deltas):
        base = ((me + delta + devices) % devices) * NB
        block = jnp.int32(0)
        place = jnp.int32(0)
        for n in range(NB):
            offset = z_dest[n] - base
            hit = jnp.logical_and(offset >= 0, offset < NB)
            block = block + jnp.where(hit, n, 0)
            place = place + jnp.where(hit, offset, 0)
        block = jnp.minimum(block, NB - 1)
        x_first[pl.ds(slot * BLK, BLK), :] = x_ref[block]
        limit = patch_len[0] - block * BLK
        meta = jnp.where(row == 1, limit, place)
        meta_send[slot] = meta
        if delta == 0:
            meta_recv[slot] = meta
    qt[...] = jnp.zeros_like(qt)
    for slot, delta in enumerate(deltas):
        if delta:
            meta_copy(slot).start()

    chunks = PATCH // ROWS
    transpose_weights(0, wqkv, wqv_t)
    for chunk in range(chunks):
        project(0, chunk, x_first, meta_send, gain, wqkv, wqv_t, kk, qt, vt)
    attention(kk, qt, vt, ot, s_a, s_b, m_a, m_b)
    for chunk in range(chunks):
        y = finish(0, chunk, x_first, gain, ot, wo, wup, wdown)
        for part in range(2):
            slot = chunk * 2 + part
            rows = pl.ds(slot * BLK, BLK)
            piece = y[part * BLK : (part + 1) * BLK, :]
            if deltas[slot]:
                y_send[rows, :] = piece
                block_copy(slot).start()
            else:
                x_second[rows, :] = piece

    transpose_weights(1, wqkv, wqv_t)
    for slot, delta in enumerate(deltas):
        if delta:
            meta_copy(slot).wait()
    for chunk in range(chunks):
        for slot in (chunk * 2, chunk * 2 + 1):
            if deltas[slot]:
                block_copy(slot).wait()
        project(1, chunk, x_second, meta_recv, gain, wqkv, wqv_t, kk, qt, vt)
    attention(kk, qt, vt, ot, s_a, s_b, m_a, m_b)

    number = lax.broadcasted_iota(jnp.int32, (POOL_ROWS, BLK), 0)
    wanted = jnp.where(number == CELL_DEV, -1, jnp.where(number > CELL_DEV, -5, number))
    lane = lax.broadcasted_iota(jnp.int32, (1, BLK), 1)
    ones = jnp.ones((ROWS, 128), bf16)
    sums = jnp.zeros((POOL_ROWS, C), f32)
    counts = jnp.zeros((POOL_ROWS, 128), f32)
    for chunk in range(chunks):
        y = finish(1, chunk, x_second, gain, ot, wo, wup, wdown)
        members = []
        for slot in (chunk * 2, chunk * 2 + 1):
            place = meta_recv[slot, 0:1, 0:BLK]
            cell = jnp.zeros((1, BLK), jnp.int32)
            for n in range(NB):
                cell = cell + jnp.where(place == n, cells[n : n + 1, :], 0)
            cell = jnp.where(lane < meta_recv[slot, 1:2, 0:BLK], cell - me * CELL_DEV, -9)
            members.append((cell == wanted).astype(f32).astype(bf16))
        member = jnp.concatenate(members, axis=1)
        sums = sums + dot(member, y)
        counts = counts + dot(member, ones)

    rim_send[:, 0:C] = sums[CELL_DEV : CELL_DEV + 8, :]
    rim_send[:, C : C + 128] = counts[CELL_DEV : CELL_DEV + 8, :]
    rim = remote(rim_send, rim_recv, rim_send_sem, rim_recv_sem, -1)
    rim.start()

    def pooled(total, count):
        count = jnp.maximum(count, 1.0)
        mean = total / jnp.concatenate([count, count], axis=1)
        return gelu(dot(mean.astype(bf16), wpool[...])).astype(bf16)

    out[...] = pooled(sums[:CELL_DEV, :], counts[:CELL_DEV, :])
    rim.wait()
    tail = CELL_DEV - 16
    last = lax.broadcasted_iota(jnp.int32, (16, 1), 0) == 15
    extra = jnp.where(last, rim_recv[0:1, 0:C], 0.0)
    extra_count = jnp.where(last, rim_recv[0:1, C : C + 128], 0.0)
    out[tail:, :] = pooled(
        sums[tail:CELL_DEV, :] + extra, counts[tail:CELL_DEV, :] + extra_count
    )


def on_device(
    points_z,
    patch_len,
    z_dest,
    cell_of,
    norm_gain,
    qkv_weight,
    out_weight,
    up_weight,
    down_weight,
    pool_weight,
):
    n_pts = lax.axis_size("pts")
    devices = lax.axis_size(("grp", "pts"))
    deltas = (3, -3, 2, -2, 1, -1, devices // 2, 0)
    vmem = pl.BlockSpec(memory_space=pltpu.VMEM)
    smem = pl.BlockSpec(memory_space=pltpu.SMEM)
    return pl.pallas_call(
        functools.partial(body, deltas, devices, n_pts),
        out_shape=jax.ShapeDtypeStruct((CELL_DEV, CP), bf16),
        in_specs=[smem, smem] + [vmem] * 8,
        out_specs=vmem,
        scratch_shapes=[
            pltpu.VMEM((PATCH, C), bf16),
            pltpu.VMEM((PATCH, C), bf16),
            pltpu.VMEM((PATCH, C), bf16),
            pltpu.VMEM((2 * C, C), bf16),
            pltpu.VMEM((2, PATCH, C), bf16),
            pltpu.VMEM((HEADS, C, PATCH), bf16),
            pltpu.VMEM((HEADS, 2 * HD, PATCH), bf16),
            pltpu.VMEM((C, PATCH), bf16),
            pltpu.VMEM((PATCH, QW), f32),
            pltpu.VMEM((PATCH, QW), f32),
            pltpu.VMEM((8, QW), f32),
            pltpu.VMEM((8, QW), f32),
            pltpu.VMEM((NB, 8, C), jnp.int32),
            pltpu.VMEM((NB, 8, C), jnp.int32),
            pltpu.VMEM((8, C + 128), f32),
            pltpu.VMEM((8, C + 128), f32),
            pltpu.SemaphoreType.DMA((NB,)),
            pltpu.SemaphoreType.DMA((NB,)),
            pltpu.SemaphoreType.DMA((NB,)),
            pltpu.SemaphoreType.DMA((NB,)),
            pltpu.SemaphoreType.DMA,
            pltpu.SemaphoreType.DMA,
        ],
        compiler_params=pltpu.CompilerParams(
            collective_id=0, has_side_effects=True, vmem_limit_bytes=48 * 2**20
        ),
        name="encoder",
    )(
        patch_len,
        z_dest,
        points_z.reshape(NB, BLK, C),
        cell_of.reshape(NB, BLK),
        norm_gain,
        qkv_weight,
        out_weight,
        up_weight,
        down_weight,
        pool_weight,
    )


def solution(mesh):
    placed = (
        P(("grp", "pts"), None),
        P(("grp", "pts")),
        P(("grp", "pts")),
        P(("grp", "pts")),
        P(),
        P(),
        P(),
        P(),
        P(),
        P(),
    )
    return jax.shard_map(
        on_device, mesh=mesh, in_specs=placed, out_specs=P(("grp", "pts"), None), check_vma=False
    )
```

time: 339 us -> 75.1 us (0.22)
  the two profiles are of different devices: /device:TPU:24 before, /device:TPU:16 now
where the time goes in v1:
time: 75.1 us; the launch traced here: 74.7 us
  Pallas kernels  65.5 us (87%)
  local copies, waits for them, and re-layouts  8.56 us (11%)
    pallas_call x1, Pallas kernels, on_device(): pl.pallas_call(functools.partial(body, deltas, devices, n_pts), out_shape...  65.5 us
    unnamed x19, local copies, waits for them, and re-layouts  8.56 us

profile of v1, /device:TPU:16, one launch (start us, length us, event | category | flops | bytes accessed | tf_op | source)
XLA Modules:
  0.0 74.7 jit_solution(867159933948580487)
XLA Ops:
  0.0 0.0 copy-start.6
  0.7 0.0 copy-start.8
  0.7 0.0 copy-done.6
  0.7 0.6 copy-done.8
  1.3 0.0 copy-start
  1.3 1.2 %copy-done = bf16[2,256,1024]{2,1,0:T(8,128)(2,1)S(1)} copy-done((bf16[2,256,1024]{2,1,0:T(8,128)(2,1)S(1)}, bf16[2,256,1024]{2,1,0:T(8,128)(2,1)}, u32[]{:S(2)}) %copy-start) | copy-done | bytes 1048600
  2.6 0.0 copy-start.1
  2.6 1.2 %copy-done.1 = bf16[2,1024,256]{2,1,0:T(8,128)(2,1)S(1)} copy-done((bf16[2,1024,256]{2,1,0:T(8,128)(2,1)S(1)}, bf16[2,1024,256]{2,1,0:T(8,128)(2,1)}, u32[]{:S(2)}) %copy-start.1) | copy-done | bytes 1048600
  3.8 0.0 copy-start.2
  3.8 1.1 %copy-done.2 = bf16[2,256,768]{2,1,0:T(8,128)(2,1)S(1)} copy-done((bf16[2,256,768]{2,1,0:T(8,128)(2,1)S(1)}, bf16[2,256,768]{2,1,0:T(8,128)(2,1)}, u32[]{:S(2)}) %copy-start.2) | copy-done | bytes 786456
  4.9 0.0 copy-start.3
  4.9 1.0 %copy-done.3 = bf16[1024,256]{1,0:T(8,128)(2,1)S(1)} copy-done((bf16[1024,256]{1,0:T(8,128)(2,1)S(1)}, bf16[1024,256]{1,0:T(8,128)(2,1)}, u32[]{:S(2)}) %copy-start.3) | copy-done | bytes 524312
  6.0 0.0 copy-start.4
  6.0 0.9 %copy-done.4 = bf16[2,256,256]{2,1,0:T(8,128)(2,1)S(1)} copy-done((bf16[2,256,256]{2,1,0:T(8,128)(2,1)S(1)}, bf16[2,256,256]{2,1,0:T(8,128)(2,1)}, u32[]{:S(2)}) %copy-start.4) | copy-done | bytes 262168
  6.9 0.0 copy-start.5
  6.9 0.9 %copy-done.5 = bf16[256,512]{1,0:T(8,128)(2,1)S(1)} copy-done((bf16[256,512]{1,0:T(8,128)(2,1)S(1)}, bf16[256,512]{1,0:T(8,128)(2,1)}, u32[]{:S(2)}) %copy-start.5) | copy-done | bytes 262168
  7.9 0.0 copy-start.7
  7.9 0.7 copy-done.7
  8.5 65.5 %encoder.1 = bf16[256,512]{1,0:T(8,128)(2,1)S(1)} custom-call(s32[1]{0:T(128)S(6)} %copy.12.patch_len, s32[8]{0:T(128)S(1)} %copy-done.8, bf16[8,128,256]{2,1,0:T(8,128)(2,1)S(1)} %bitcast.2, s32[8,128]{1,0:T(8,128)S(1)} %bitcast.3, f32[2,2,256]{2,1,0:T(2,128)S(1)} %copy-done.7, bf16[2,256,768]{2,1,0:T(8,128)(2,1)S(1)} %copy-done.2, ...), custom_call_target="tpu_custom_call" | custom-call | tf_op jit(solution)/shard_map/encoder/pallas_call | solution.py:326
  74.0 0.7 copy.13
Async XLA Ops:
  0.0 0.7 copy-start.6
  0.7 0.7 copy-start.8
  1.3 1.2 %copy-start = (bf16[2,256,1024]{2,1,0:T(8,128)(2,1)S(1)}, bf16[2,256,1024]{2,1,0:T(8,128)(2,1)}, u32[]{:S(2)}) copy-start(bf16[2,256,1024]{2,1,0:T(8,128)(2,1)} %wup.1) | copy-start | bytes 3145732
  2.6 1.2 %copy-start.1 = (bf16[2,1024,256]{2,1,0:T(8,128)(2,1)S(1)}, bf16[2,1024,256]{2,1,0:T(8,128)(2,1)}, u32[]{:S(2)}) copy-start(bf16[2,1024,256]{2,1,0:T(8,128)(2,1)} %wdown.1) | copy-start | bytes 3145732
  3.8 1.1 %copy-start.2 = (bf16[2,256,768]{2,1,0:T(8,128)(2,1)S(1)}, bf16[2,256,768]{2,1,0:T(8,128)(2,1)}, u32[]{:S(2)}) copy-start(bf16[2,256,768]{2,1,0:T(8,128)(2,1)} %wqkv.1) | copy-start | bytes 2359300
  4.9 1.0 %copy-start.3 = (bf16[1024,256]{1,0:T(8,128)(2,1)S(1)}, bf16[1024,256]{1,0:T(8,128)(2,1)}, u32[]{:S(2)}) copy-start(bf16[1024,256]{1,0:T(8,128)(2,1)} %param.10) | copy-start | bytes 1572868
  6.0 0.9 %copy-start.4 = (bf16[2,256,256]{2,1,0:T(8,128)(2,1)S(1)}, bf16[2,256,256]{2,1,0:T(8,128)(2,1)}, u32[]{:S(2)}) copy-start(bf16[2,256,256]{2,1,0:T(8,128)(2,1)} %wo.1) | copy-start | bytes 786436
  6.9 0.9 %copy-start.5 = (bf16[256,512]{1,0:T(8,128)(2,1)S(1)}, bf16[256,512]{1,0:T(8,128)(2,1)}, u32[]{:S(2)}) copy-start(bf16[256,512]{1,0:T(8,128)(2,1)} %wpool.1) | copy-start | bytes 786436
  7.9 0.7 copy-start.7

commit v2 on v1

--- a/solution.py
+++ b/solution.py
@@ -22,23 +22,23 @@
 LOG2E = 1.4426950408889634
 POOL_ROWS = 272
 ERF = (
-    0.7978722361090334,
-    0.03636660609986694,
-    -5.8514434084682766e-05,
-    -4.7090980998381986e-05,
-    2.779316469575001e-06,
-    -5.589976858483281e-08,
+    0.7978281360364785,
+    0.03646879080750627,
+    -0.00012486153426078468,
+    -3.0581026877848916e-05,
+    1.1190833948473977e-06,
 )
-ERF_END = 5.6 * 5.6
+F8_TOP = 400.0
 bf16 = jnp.bfloat16
+f8 = jnp.float8_e4m3fn
 f32 = jnp.float32
 MESH = pl.DeviceIdType.MESH
 
 
 def gelu(x):
-    u = jnp.minimum(x * x, ERF_END)
-    r = ERF[5]
-    for coefficient in ERF[4::-1]:
+    u = x * x
+    r = ERF[4]
+    for coefficient in ERF[3::-1]:
         r = r * u + coefficient
     half = 0.5 * x
     return half + half * jnp.tanh(x * r)
@@ -62,61 +62,98 @@
     return lax.dot_general(a, b, (((0,), (0,)), ((), ())), preferred_element_type=f32)
 
 
-def project(b, chunk, xs, meta, gain, wqkv, wqv_t, kk, qt, vt):
+def prepare(b, gain, wqkv, wq_t, wk2, sigma):
+    reach = 16.1 * jnp.max(jnp.abs(gain[b, 0:1, :]))
+    column = lax.broadcasted_iota(jnp.int32, (C, C), 0) // HD
+    same_head = (column == lax.broadcasted_iota(jnp.int32, (C, C), 1) // HD).astype(f32).astype(bf16)
+
+    def power(exponent):
+        return jnp.exp2(exponent).astype(bf16).astype(f32)
+
+    def exponents(w):
+        squares = jnp.sum(w * w, axis=0, keepdims=True)
+        squares = jnp.broadcast_to(squares, (16, C)).astype(bf16)
+        total = jnp.maximum(dot(squares, same_head)[0:1, :], 1e-30)
+        bound = reach * jnp.sqrt(total)
+        return jnp.floor(jnp.log(F8_TOP / bound) * LOG2E)
+
+    wq = wqkv[b, :, 0:C].astype(f32)
+    wk = wqkv[b, :, C : 2 * C].astype(f32)
+    wv = wqkv[b, :, 2 * C : 3 * C].astype(f32)
+    q_up, k_up = exponents(wq), exponents(wk)
+    wq_t[0:C, :] = (wq * power(q_up)).T.astype(bf16)
+    wq_t[C : 2 * C, :] = wv.T.astype(bf16)
+    column = lax.broadcasted_iota(jnp.int32, (C, 2 * C), 0)
+    wide = lax.broadcasted_iota(jnp.int32, (C, 2 * C), 1)
+    twice = (column == (wide // (2 * HD)) * HD + wide % HD).astype(f32).astype(bf16)
+    wk2[...] = dot((wk * power(k_up)).astype(bf16), twice).astype(bf16)
+    back = power(-q_up - k_up) * (HD**-0.5 * LOG2E)
+    for h in range(HEADS):
+        sigma[h] = jnp.broadcast_to(back[:, h * HD : h * HD + 1], (8, QW))
+
+
+def project(b, chunk, xs, meta, gain, wq_t, wk2, kk, qt, vt, spare):
     rows = pl.ds(chunk * ROWS, ROWS)
     xn = norm(xs[rows, :].astype(f32), gain[b, 0:1, :])
-    k = dot(xn, wqkv[b, :, C : 2 * C])
+    k = dot(xn, wk2[...]).astype(bf16).astype(f32)
+    is_high = lax.broadcasted_iota(jnp.int32, (BLK, 2 * C), 1) % (2 * HD) < HD
     for part in range(2):
         slot = chunk * 2 + part
         limit = meta[slot, 1:2, :]
-        live = lax.broadcasted_iota(jnp.int32, (BLK, C), 0) < limit
+        limit = jnp.concatenate([limit, limit], axis=1)
+        spare[slot : slot + 1, :] = (BLK - jnp.minimum(limit, BLK)).astype(f32)
+        live = lax.broadcasted_iota(jnp.int32, (BLK, 2 * C), 0) < limit
         piece = k[part * BLK : (part + 1) * BLK, :]
-        piece = jnp.where(live, piece, piece[0:1, :]).astype(bf16)
-        at = pl.ds(slot * BLK, BLK)
-        for g in range(2):
-            lanes = piece[:, g * 128 : (g + 1) * 128]
-            kk[g, at, 0:128] = lanes
-            kk[g, at, 128:256] = lanes
-    qv = dot_nt(wqv_t[...], xn)
-    q = qv[:C, :].astype(bf16).astype(f32) * (HD**-0.5 * LOG2E)
-    hi = q.astype(bf16)
-    lo = (q - hi.astype(f32)).astype(bf16)
+        piece = jnp.where(live, piece, piece[0:1, :])
+        high = piece.astype(f8).astype(f32)
+        piece = jnp.where(is_high, high, piece - high).astype(f8)
+        for g in range(4):
+            kk[g, pl.ds(slot * BLK, BLK), :] = piece[:, g * 128 : (g + 1) * 128]
+    qv = dot_nt(wq_t[...], xn)
+    q = qv[:C, :].astype(bf16).astype(f32)
+    high = q.astype(f8).astype(f32)
+    low = q - high
     for h in range(HEADS):
-        r = (h % 8) * HD
-        qt[h, r : r + HD, rows] = hi[h * HD : (h + 1) * HD, :]
-        qt[h, 128 + r : 128 + r + HD, rows] = lo[h * HD : (h + 1) * HD, :]
+        r = (h % 4) * 2 * HD
+        at = slice(h * HD, (h + 1) * HD)
+        qt[h, r : r + 2 * HD, rows] = jnp.concatenate([high[at], high[at]], axis=0).astype(f8)
+        qt[h, 128 + r : 128 + r + 2 * HD, rows] = jnp.concatenate(
+            [low[at], low[at]], axis=0
+        ).astype(f8)
     limits = jnp.concatenate(
         [meta[chunk * 2, 1:2, 0:BLK], meta[chunk * 2 + 1, 1:2, 0:BLK]], axis=1
     )
     lane = lax.broadcasted_iota(jnp.int32, (1, ROWS), 1) % BLK
-    live_row = (lane < limits).astype(f32)
-    v = (qv[C:, :] * live_row).astype(bf16)
-    first = lax.broadcasted_iota(jnp.int32, (HD, ROWS), 0) == 0
-    ones = jnp.where(first, live_row, 0.0).astype(bf16)
+    v = (qv[C:, :] * (lane < limits).astype(f32)).astype(bf16)
     for h in range(HEADS):
-        vt[h, 0:HD, rows] = v[h * HD : (h + 1) * HD, :]
-        vt[h, HD : 2 * HD, rows] = ones
-
-
-def attention(kk, qt, vt, ot, s_a, s_b, m_a, m_b):
+        vt[h, :, rows] = v[h * HD : (h + 1) * HD, :]
+
+
+def attention(kk, qt, vt, ot, sigma, spare, s_a, s_b, m_a, m_b):
     tiles = PATCH // QW
 
     def scores(h, t, s, m):
-        raw = dot(kk[h // 8], qt[h, :, pl.ds(t * QW, QW)])
+        keys = kk[h // 4]
+        raw = dot(jnp.concatenate([keys, keys], axis=1), qt[h, :, pl.ds(t * QW, QW)])
         s[...] = raw
         m[...] = jnp.max(raw.reshape(PATCH // 8, 8, QW), axis=0)
 
     def values(h, t, s, m):
-        top = jnp.max(m[...], axis=0, keepdims=True)
+        scale = sigma[h][0:1, :]
+        top = jnp.max(m[...], axis=0, keepdims=True) * scale
         total = None
         for c in range(PATCH // 256):
             keys = pl.ds(c * 256, 256)
-            e = jnp.exp2(s[keys, :] - top).astype(bf16)
-            part = dot(vt[h, :, keys], e)
-            total = part if total is None else total + part
-        ot[pl.ds(pl.multiple_of(h * HD, HD), HD), pl.ds(t * QW, QW)] = (
-            total[0:HD, :] / total[HD : HD + 1, :]
-        ).astype(bf16)
+            e = jnp.exp2(s[keys, :] * scale - top)
+            part = dot(vt[h, :, keys], e.astype(bf16))
+            count = jnp.sum(e.reshape(32, 8, QW), axis=0)
+            over = spare[2 * c : 2 * c + 1, :] * e[0:1] + spare[2 * c + 1 : 2 * c + 2, :] * e[BLK : BLK + 1]
+            if total is None:
+                total, counted, left_out = part, count, over
+            else:
+                total, counted, left_out = total + part, counted + count, left_out + over
+        den = jnp.sum(counted, axis=0, keepdims=True) - left_out
+        ot[pl.ds(pl.multiple_of(h * HD, HD), HD), pl.ds(t * QW, QW)] = (total / den).astype(bf16)
 
     scores(0, 0, s_a, m_a)
 
@@ -132,19 +169,17 @@
     lax.fori_loop(0, HEADS, head, 0)
 
 
-def finish(b, chunk, xs, gain, ot, wo, wup, wdown):
+def residual(b, chunk, xs, gain, ot, wo, hs, hns):
     rows = pl.ds(chunk * ROWS, ROWS)
-    h = xs[rows, :].astype(f32) + dot_tn(ot[:, rows], wo[b])
-    h = h.astype(bf16).astype(f32)
-    hn = norm(h, gain[b, 1:2, :])
-    u = gelu(dot(hn, wup[b])).astype(bf16)
-    return (h + dot(u, wdown[b])).astype(bf16)
-
-
-def transpose_weights(b, wqkv, wqv_t):
-    for part, first in enumerate((0, 2 * C)):
-        w = wqkv[b, :, first : first + C].astype(f32)
-        wqv_t[part * C : (part + 1) * C, :] = w.T.astype(bf16)
+    h = (xs[rows, :].astype(f32) + dot_tn(ot[:, rows], wo[b])).astype(bf16)
+    hs[rows, :] = h
+    hns[rows, :] = norm(h.astype(f32), gain[b, 1:2, :])
+
+
+def feed_forward(b, chunk, hs, hns, wup, wdown):
+    rows = pl.ds(chunk * ROWS, ROWS)
+    u = gelu(dot(hns[rows, :], wup[b])).astype(bf16)
+    return (hs[rows, :].astype(f32) + dot(u, wdown[b])).astype(bf16)
 
 
 def body(
@@ -153,6 +188,15 @@
     n_pts,
     patch_len,
     z_dest,
+    x_hbm,
+    cells_hbm,
+    gain_hbm,
+    wqkv_hbm,
+    wo_hbm,
+    wup_hbm,
+    wdown_hbm,
+    wpool_hbm,
+    out,
     x_ref,
     cells,
     gain,
@@ -161,11 +205,15 @@
     wup,
     wdown,
     wpool,
-    out,
+    hs,
+    hns,
+    sigma,
+    spare,
     x_first,
     x_second,
     y_send,
-    wqv_t,
+    wq_t,
+    wk2,
     kk,
     qt,
     vt,
@@ -184,7 +232,25 @@
     meta_recv_sem,
     rim_send_sem,
     rim_recv_sem,
+    load_sem,
 ):
+    loads = [
+        pltpu.make_async_copy(src, dst, load_sem.at[n])
+        for n, (src, dst) in enumerate(
+            (
+                (x_hbm, x_ref),
+                (gain_hbm, gain),
+                (wqkv_hbm, wqkv),
+                (wo_hbm, wo),
+                (wup_hbm, wup),
+                (wdown_hbm, wdown),
+                (cells_hbm, cells),
+                (wpool_hbm, wpool),
+            )
+        )
+    ]
+    for load in loads:
+        load.start()
     me = lax.axis_index("grp") * n_pts + lax.axis_index("pts")
 
     def device(delta):
@@ -215,6 +281,9 @@
             meta_recv_sem.at[slot], deltas[slot],
         )
 
+    qt[...] = jnp.zeros_like(qt)
+    for load in loads[:3]:
+        load.wait()
     row = lax.broadcasted_iota(jnp.int32, (8, C), 0)
     for slot, delta in enumerate(deltas):
         base = ((me + delta + devices) % devices) * NB
@@ -232,18 +301,21 @@
         meta_send[slot] = meta
         if delta == 0:
             meta_recv[slot] = meta
-    qt[...] = jnp.zeros_like(qt)
     for slot, delta in enumerate(deltas):
         if delta:
             meta_copy(slot).start()
 
     chunks = PATCH // ROWS
-    transpose_weights(0, wqkv, wqv_t)
-    for chunk in range(chunks):
-        project(0, chunk, x_first, meta_send, gain, wqkv, wqv_t, kk, qt, vt)
-    attention(kk, qt, vt, ot, s_a, s_b, m_a, m_b)
-    for chunk in range(chunks):
-        y = finish(0, chunk, x_first, gain, ot, wo, wup, wdown)
+    prepare(0, gain, wqkv, wq_t, wk2, sigma)
+    for chunk in range(chunks):
+        project(0, chunk, x_first, meta_send, gain, wq_t, wk2, kk, qt, vt, spare)
+    attention(kk, qt, vt, ot, sigma, spare, s_a, s_b, m_a, m_b)
+    for load in loads[3:]:
+        load.wait()
+    for chunk in range(chunks):
+        residual(0, chunk, x_first, gain, ot, wo, hs, hns)
+    for chunk in range(chunks):
+        y = feed_forward(0, chunk, hs, hns, wup, wdown)
         for part in range(2):
             slot = chunk * 2 + part
             rows = pl.ds(slot * BLK, BLK)
@@ -254,7 +326,7 @@
             else:
                 x_second[rows, :] = piece
 
-    transpose_weights(1, wqkv, wqv_t)
+    prepare(1, gain, wqkv, wq_t, wk2, sigma)
     for slot, delta in enumerate(deltas):
         if delta:
             meta_copy(slot).wait()
@@ -262,8 +334,10 @@
         for slot in (chunk * 2, chunk * 2 + 1):
             if deltas[slot]:
                 block_copy(slot).wait()
-        project(1, chunk, x_second, meta_recv, gain, wqkv, wqv_t, kk, qt, vt)
-    attention(kk, qt, vt, ot, s_a, s_b, m_a, m_b)
+        project(1, chunk, x_second, meta_recv, gain, wq_t, wk2, kk, qt, vt, spare)
+    attention(kk, qt, vt, ot, sigma, spare, s_a, s_b, m_a, m_b)
+    for chunk in range(chunks):
+        residual(1, chunk, x_second, gain, ot, wo, hs, hns)
 
     number = lax.broadcasted_iota(jnp.int32, (POOL_ROWS, BLK), 0)
     wanted = jnp.where(number == CELL_DEV, -1, jnp.where(number > CELL_DEV, -5, number))
@@ -272,7 +346,7 @@
     sums = jnp.zeros((POOL_ROWS, C), f32)
     counts = jnp.zeros((POOL_ROWS, 128), f32)
     for chunk in range(chunks):
-        y = finish(1, chunk, x_second, gain, ot, wo, wup, wdown)
+        y = feed_forward(1, chunk, hs, hns, wup, wdown)
         members = []
         for slot in (chunk * 2, chunk * 2 + 1):
             place = meta_recv[slot, 0:1, 0:BLK]
@@ -326,16 +400,29 @@
     return pl.pallas_call(
         functools.partial(body, deltas, devices, n_pts),
         out_shape=jax.ShapeDtypeStruct((CELL_DEV, CP), bf16),
-        in_specs=[smem, smem] + [vmem] * 8,
+        in_specs=[smem, smem] + [pl.BlockSpec(memory_space=pl.ANY)] * 8,
         out_specs=vmem,
         scratch_shapes=[
+            pltpu.VMEM((NB, BLK, C), bf16),
+            pltpu.VMEM((NB, BLK), jnp.int32),
+            pltpu.VMEM((2, 2, C), f32),
+            pltpu.VMEM((2, C, 3 * C), bf16),
+            pltpu.VMEM((2, C, C), bf16),
+            pltpu.VMEM((2, C, FF), bf16),
+            pltpu.VMEM((2, FF, C), bf16),
+            pltpu.VMEM((C, CP), bf16),
+            pltpu.VMEM((PATCH, C), bf16),
+            pltpu.VMEM((PATCH, C), bf16),
+            pltpu.VMEM((HEADS, 8, QW), f32),
+            pltpu.VMEM((NB, QW), f32),
             pltpu.VMEM((PATCH, C), bf16),
             pltpu.VMEM((PATCH, C), bf16),
             pltpu.VMEM((PATCH, C), bf16),
             pltpu.VMEM((2 * C, C), bf16),
-            pltpu.VMEM((2, PATCH, C), bf16),
-            pltpu.VMEM((HEADS, C, PATCH), bf16),
-            pltpu.VMEM((HEADS, 2 * HD, PATCH), bf16),
+            pltpu.VMEM((C, 2 * C), bf16),
+            pltpu.VMEM((4, PATCH, 128), f8),
+            pltpu.VMEM((HEADS, C, PATCH), f8),
+            pltpu.VMEM((HEADS, HD, PATCH), bf16),
             pltpu.VMEM((C, PATCH), bf16),
             pltpu.VMEM((PATCH, QW), f32),
             pltpu.VMEM((PATCH, QW), f32),
@@ -351,9 +438,10 @@
             pltpu.SemaphoreType.DMA((NB,)),
             pltpu.SemaphoreType.DMA,
             pltpu.SemaphoreType.DMA,
+            pltpu.SemaphoreType.DMA((8,)),
         ],
         compiler_params=pltpu.CompilerParams(
-            collective_id=0, has_side_effects=True, vmem_limit_bytes=48 * 2**20
+            collective_id=0, has_side_effects=True, vmem_limit_bytes=60 * 2**20
         ),
         name="encoder",
     )(

time: 75.1 us -> 64.3 us (0.86)
  the two profiles are of different devices: /device:TPU:16 before, /device:TPU:1 now
where the time goes in v2:
time: 64.3 us; the launch traced here: 63.1 us
  Pallas kernels  60.8 us (95%)
  local copies, waits for them, and re-layouts  1.67 us (3%)
  between operations  0.66 us (1%)
    pallas_call x1, Pallas kernels, on_device(): pl.pallas_call(functools.partial(body, deltas, devices, n_pts), out_shape...  60.8 us
    unnamed x1, local copies, waits for them, and re-layouts  1.67 us

profile of v2, /device:TPU:1, one launch (start us, length us, event | category | flops | bytes accessed | tf_op | source)
XLA Modules:
  0.0 63.1 jit_solution(978479651137741291)
XLA Ops:
  0.7 60.8 %encoder.1 = bf16[256,512]{1,0:T(8,128)(2,1)} custom-call(s32[1]{0:T(128)S(6)} %copy.12.patch_len, s32[8]{0:T(128)} %z_dest.1, bf16[8,128,256]{2,1,0:T(8,128)(2,1)} %bitcast.2, s32[8,128]{1,0:T(8,128)} %bitcast.3, f32[2,2,256]{2,1,0:T(2,128)} %gain_hbm.1, bf16[2,256,768]{2,1,0:T(8,128)(2,1)} %wqkv_hbm.1, bf16[2,256,256]{2,1,0:T(8,128)(2,1)} %wo_hbm.1, ...), custom_call_target="tpu_custom_call" | custom-call | tf_op jit(solution)/shard_map/encoder/pallas_call | solution.py:400
  61.5 1.7 %copy.13 = bf16[256,512]{1,0:T(8,128)(2,1)} copy(bf16[256,512]{1,0:T(8,128)(2,1)} %encoder.1) | data formatting | bytes 524288

commit v3 on v2

--- a/solution.py
+++ b/solution.py
@@ -18,6 +18,7 @@
 FF = 1024
 NORM_EPS = 1e-05
 QW = 512
+TILES = PATCH // QW
 ROWS = 256
 LOG2E = 1.4426950408889634
 POOL_ROWS = 272
@@ -92,7 +93,7 @@
         sigma[h] = jnp.broadcast_to(back[:, h * HD : h * HD + 1], (8, QW))
 
 
-def project(b, chunk, xs, meta, gain, wq_t, wk2, kk, qt, vt, spare):
+def project(b, chunk, xs, meta, gain, wq_t, wk2, kk, qt, vt):
     rows = pl.ds(chunk * ROWS, ROWS)
     xn = norm(xs[rows, :].astype(f32), gain[b, 0:1, :])
     k = dot(xn, wk2[...]).astype(bf16).astype(f32)
@@ -101,7 +102,6 @@
         slot = chunk * 2 + part
         limit = meta[slot, 1:2, :]
         limit = jnp.concatenate([limit, limit], axis=1)
-        spare[slot : slot + 1, :] = (BLK - jnp.minimum(limit, BLK)).astype(f32)
         live = lax.broadcasted_iota(jnp.int32, (BLK, 2 * C), 0) < limit
         piece = k[part * BLK : (part + 1) * BLK, :]
         piece = jnp.where(live, piece, piece[0:1, :])
@@ -124,49 +124,51 @@
         [meta[chunk * 2, 1:2, 0:BLK], meta[chunk * 2 + 1, 1:2, 0:BLK]], axis=1
     )
     lane = lax.broadcasted_iota(jnp.int32, (1, ROWS), 1) % BLK
-    v = (qv[C:, :] * (lane < limits).astype(f32)).astype(bf16)
+    live_row = (lane < limits).astype(f32)
+    v = (qv[C:, :] * live_row).astype(bf16)
+    first = lax.broadcasted_iota(jnp.int32, (HD, ROWS), 0) == 0
+    ones = jnp.where(first, live_row, 0.0).astype(bf16)
     for h in range(HEADS):
-        vt[h, :, rows] = v[h * HD : (h + 1) * HD, :]
-
-
-def attention(kk, qt, vt, ot, sigma, spare, s_a, s_b, m_a, m_b):
-    tiles = PATCH // QW
-
-    def scores(h, t, s, m):
-        keys = kk[h // 4]
-        raw = dot(jnp.concatenate([keys, keys], axis=1), qt[h, :, pl.ds(t * QW, QW)])
-        s[...] = raw
-        m[...] = jnp.max(raw.reshape(PATCH // 8, 8, QW), axis=0)
-
-    def values(h, t, s, m):
-        scale = sigma[h][0:1, :]
-        top = jnp.max(m[...], axis=0, keepdims=True) * scale
-        total = None
-        for c in range(PATCH // 256):
-            keys = pl.ds(c * 256, 256)
-            e = jnp.exp2(s[keys, :] * scale - top)
-            part = dot(vt[h, :, keys], e.astype(bf16))
-            count = jnp.sum(e.reshape(32, 8, QW), axis=0)
-            over = spare[2 * c : 2 * c + 1, :] * e[0:1] + spare[2 * c + 1 : 2 * c + 2, :] * e[BLK : BLK + 1]
-            if total is None:
-                total, counted, left_out = part, count, over
-            else:
-                total, counted, left_out = total + part, counted + count, left_out + over
-        den = jnp.sum(counted, axis=0, keepdims=True) - left_out
-        ot[pl.ds(pl.multiple_of(h * HD, HD), HD), pl.ds(t * QW, QW)] = (total / den).astype(bf16)
-
-    scores(0, 0, s_a, m_a)
-
-    def head(h, carry):
-        for t in range(tiles):
-            now = (s_a, m_a) if t % 2 == 0 else (s_b, m_b)
-            later = (s_b, m_b) if t % 2 == 0 else (s_a, m_a)
-            next_h = h if t < tiles - 1 else jnp.minimum(h + 1, HEADS - 1)
-            scores(next_h, (t + 1) % tiles, *later)
-            values(h, t, *now)
+        vt[h, 0:HD, rows] = v[h * HD : (h + 1) * HD, :]
+        vt[h, HD : 2 * HD, rows] = ones
+
+
+def scores(step, kk, qt, sigma, s, m):
+    h, t = step % HEADS, step // HEADS
+    keys = kk[h // 4]
+    queries = qt[h, :, pl.ds(pl.multiple_of(t * QW, QW), QW)]
+    raw = dot(jnp.concatenate([keys, keys], axis=1), queries) * sigma[h][0:1, :]
+    s[...] = raw
+    m[...] = jnp.max(raw.reshape(PATCH // 8, 8, QW), axis=0)
+
+
+def values(h, t, vt, ot, s, m):
+    top = jnp.max(m[...], axis=0, keepdims=True)
+    total = None
+    for c in range(PATCH // 256):
+        keys = pl.ds(c * 256, 256)
+        e = jnp.exp2(s[keys, :] - top).astype(bf16)
+        part = dot(vt[h, :, keys], e)
+        total = part if total is None else total + part
+    ot[pl.ds(pl.multiple_of(h * HD, HD), HD), pl.ds(t * QW, QW)] = (
+        total[0:HD, :] / total[HD : HD + 1, :]
+    ).astype(bf16)
+
+
+def attention(t, kk, qt, vt, ot, sigma, s_a, s_b, m_a, m_b):
+    if t == 0:
+        scores(0, kk, qt, sigma, s_a, m_a)
+
+    def pair(n, carry):
+        h = 2 * n
+        step = t * HEADS + h
+        scores(step + 1, kk, qt, sigma, s_b, m_b)
+        values(h, t, vt, ot, s_a, m_a)
+        scores(jnp.minimum(step + 2, TILES * HEADS - 1), kk, qt, sigma, s_a, m_a)
+        values(h + 1, t, vt, ot, s_b, m_b)
         return carry
 
-    lax.fori_loop(0, HEADS, head, 0)
+    lax.fori_loop(0, HEADS // 2, pair, 0)
 
 
 def residual(b, chunk, xs, gain, ot, wo, hs, hns):
@@ -208,7 +210,6 @@
     hs,
     hns,
     sigma,
-    spare,
     x_first,
     x_second,
     y_send,
@@ -261,7 +262,6 @@
     for delta in deltas:
         if delta:
             pl.semaphore_signal(barrier, inc=1, device_id=device(delta), device_id_type=MESH)
-    pl.semaphore_wait(barrier, NB - 1)
 
     def remote(src, dst, ssem, rsem, delta):
         return pltpu.make_async_remote_copy(
@@ -301,30 +301,34 @@
         meta_send[slot] = meta
         if delta == 0:
             meta_recv[slot] = meta
+    chunks = PATCH // ROWS
+    prepare(0, gain, wqkv, wq_t, wk2, sigma)
+    for chunk in range(chunks):
+        project(0, chunk, x_first, meta_send, gain, wq_t, wk2, kk, qt, vt)
+    pl.semaphore_wait(barrier, NB - 1)
     for slot, delta in enumerate(deltas):
         if delta:
             meta_copy(slot).start()
-
-    chunks = PATCH // ROWS
-    prepare(0, gain, wqkv, wq_t, wk2, sigma)
-    for chunk in range(chunks):
-        project(0, chunk, x_first, meta_send, gain, wq_t, wk2, kk, qt, vt, spare)
-    attention(kk, qt, vt, ot, sigma, spare, s_a, s_b, m_a, m_b)
-    for load in loads[3:]:
-        load.wait()
-    for chunk in range(chunks):
-        residual(0, chunk, x_first, gain, ot, wo, hs, hns)
-    for chunk in range(chunks):
-        y = feed_forward(0, chunk, hs, hns, wup, wdown)
-        for part in range(2):
-            slot = chunk * 2 + part
-            rows = pl.ds(slot * BLK, BLK)
-            piece = y[part * BLK : (part + 1) * BLK, :]
-            if deltas[slot]:
-                y_send[rows, :] = piece
-                block_copy(slot).start()
-            else:
-                x_second[rows, :] = piece
+    per_tile = chunks // TILES
+    for t in range(TILES):
+        attention(t, kk, qt, vt, ot, sigma, s_a, s_b, m_a, m_b)
+        if t == 0:
+            for load in loads[3:]:
+                load.wait()
+        mine = range(t * per_tile, (t + 1) * per_tile)
+        for chunk in mine:
+            residual(0, chunk, x_first, gain, ot, wo, hs, hns)
+        for chunk in mine:
+            y = feed_forward(0, chunk, hs, hns, wup, wdown)
+            for part in range(2):
+                slot = chunk * 2 + part
+                rows = pl.ds(slot * BLK, BLK)
+                piece = y[part * BLK : (part + 1) * BLK, :]
+                if deltas[slot]:
+                    y_send[rows, :] = piece
+                    block_copy(slot).start()
+                else:
+                    x_second[rows, :] = piece
 
     prepare(1, gain, wqkv, wq_t, wk2, sigma)
     for slot, delta in enumerate(deltas):
@@ -334,8 +338,9 @@
         for slot in (chunk * 2, chunk * 2 + 1):
             if deltas[slot]:
                 block_copy(slot).wait()
-        project(1, chunk, x_second, meta_recv, gain, wq_t, wk2, kk, qt, vt, spare)
-    attention(kk, qt, vt, ot, sigma, spare, s_a, s_b, m_a, m_b)
+        project(1, chunk, x_second, meta_recv, gain, wq_t, wk2, kk, qt, vt)
+    for t in range(TILES):
+        attention(t, kk, qt, vt, ot, sigma, s_a, s_b, m_a, m_b)
     for chunk in range(chunks):
         residual(1, chunk, x_second, gain, ot, wo, hs, hns)
 
@@ -414,7 +419,6 @@
             pltpu.VMEM((PATCH, C), bf16),
             pltpu.VMEM((PATCH, C), bf16),
             pltpu.VMEM((HEADS, 8, QW), f32),
-            pltpu.VMEM((NB, QW), f32),
             pltpu.VMEM((PATCH, C), bf16),
             pltpu.VMEM((PATCH, C), bf16),
             pltpu.VMEM((PATCH, C), bf16),
@@ -422,7 +426,7 @@
             pltpu.VMEM((C, 2 * C), bf16),
             pltpu.VMEM((4, PATCH, 128), f8),
             pltpu.VMEM((HEADS, C, PATCH), f8),
-            pltpu.VMEM((HEADS, HD, PATCH), bf16),
+            pltpu.VMEM((HEADS, 2 * HD, PATCH), bf16),
             pltpu.VMEM((C, PATCH), bf16),
             pltpu.VMEM((PATCH, QW), f32),
             pltpu.VMEM((PATCH, QW), f32),

time: 64.3 us -> 60.3 us (0.938); the launches traced: 63.1 us -> 60.2 us
  Pallas kernels: 60.8 us -> 57.8 us
    pallas_call x1, Pallas kernels: 60.8 us -> 57.8 us  [on_device(): pl.pallas_call(functools.partial(body, deltas, devices, n_pts), out_shape...]
where the time goes in v3:
time: 60.3 us; the launch traced here: 60.2 us
  Pallas kernels  57.8 us (96%)
  local copies, waits for them, and re-layouts  1.67 us (3%)
  between operations  0.66 us (1%)
    pallas_call x1, Pallas kernels, on_device(): pl.pallas_call(functools.partial(body, deltas, devices, n_pts), out_shape...  57.8 us
    unnamed x1, local copies, waits for them, and re-layouts  1.67 us

profile of v3, /device:TPU:1, one launch (start us, length us, event | category | flops | bytes accessed | tf_op | source)
XLA Modules:
  0.0 60.2 jit_solution(4175086286170089163)
XLA Ops:
  0.7 57.8 %encoder.1 = bf16[256,512]{1,0:T(8,128)(2,1)} custom-call(s32[1]{0:T(128)S(6)} %copy.12.patch_len, s32[8]{0:T(128)} %z_dest.1, bf16[8,128,256]{2,1,0:T(8,128)(2,1)} %bitcast.2, s32[8,128]{1,0:T(8,128)} %bitcast.3, f32[2,2,256]{2,1,0:T(2,128)} %gain_hbm.1, bf16[2,256,768]{2,1,0:T(8,128)(2,1)} %wqkv_hbm.1, bf16[2,256,256]{2,1,0:T(8,128)(2,1)} %wo_hbm.1, ...), custom_call_target="tpu_custom_call" | custom-call | tf_op jit(solution)/shard_map/encoder/pallas_call | solution.py:405
  58.5 1.7 %copy.13 = bf16[256,512]{1,0:T(8,128)(2,1)} copy(bf16[256,512]{1,0:T(8,128)(2,1)} %encoder.1) | data formatting | bytes 524288

commit v4 on v3

--- a/solution.py
+++ b/solution.py
@@ -19,6 +19,7 @@
 NORM_EPS = 1e-05
 QW = 512
 TILES = PATCH // QW
+UNROLL = 8
 ROWS = 256
 LOG2E = 1.4426950408889634
 POOL_ROWS = 272
@@ -159,16 +160,17 @@
     if t == 0:
         scores(0, kk, qt, sigma, s_a, m_a)
 
-    def pair(n, carry):
-        h = 2 * n
-        step = t * HEADS + h
-        scores(step + 1, kk, qt, sigma, s_b, m_b)
-        values(h, t, vt, ot, s_a, m_a)
-        scores(jnp.minimum(step + 2, TILES * HEADS - 1), kk, qt, sigma, s_a, m_a)
-        values(h + 1, t, vt, ot, s_b, m_b)
+    def group(n, carry):
+        for o in range(0, UNROLL, 2):
+            h = UNROLL * n + o
+            step = t * HEADS + h
+            scores(step + 1, kk, qt, sigma, s_b, m_b)
+            values(h, t, vt, ot, s_a, m_a)
+            scores(jnp.minimum(step + 2, TILES * HEADS - 1), kk, qt, sigma, s_a, m_a)
+            values(h + 1, t, vt, ot, s_b, m_b)
         return carry
 
-    lax.fori_loop(0, HEADS // 2, pair, 0)
+    lax.fori_loop(0, HEADS // UNROLL, group, 0)
 
 
 def residual(b, chunk, xs, gain, ot, wo, hs, hns):

time: 60.3 us -> 57.6 us (0.955)
  Pallas kernels: 57.8 us -> 55.1 us
    pallas_call x1, Pallas kernels: 57.8 us -> 55.1 us  [on_device(): pl.pallas_call(functools.partial(body, deltas, devices, n_pts), out_shape...]
where the time goes in v4:
time: 57.6 us; the launch traced here: 57.4 us
  Pallas kernels  55.1 us (96%)
  local copies, waits for them, and re-layouts  1.67 us (3%)
  between operations  0.66 us (1%)
    pallas_call x1, Pallas kernels, on_device(): pl.pallas_call(functools.partial(body, deltas, devices, n_pts), out_shape...  55.1 us
    unnamed x1, local copies, waits for them, and re-layouts  1.67 us

profile of v4, /device:TPU:1, one launch (start us, length us, event | category | flops | bytes accessed | tf_op | source)
XLA Modules:
  0.0 57.4 jit_solution(15768296599948245170)
XLA Ops:
  0.7 55.1 %encoder.1 = bf16[256,512]{1,0:T(8,128)(2,1)} custom-call(s32[1]{0:T(128)S(6)} %copy.12.patch_len, s32[8]{0:T(128)} %z_dest.1, bf16[8,128,256]{2,1,0:T(8,128)(2,1)} %bitcast.2, s32[8,128]{1,0:T(8,128)} %bitcast.3, f32[2,2,256]{2,1,0:T(2,128)} %gain_hbm.1, bf16[2,256,768]{2,1,0:T(8,128)(2,1)} %wqkv_hbm.1, bf16[2,256,256]{2,1,0:T(8,128)(2,1)} %wo_hbm.1, ...), custom_call_target="tpu_custom_call" | custom-call | tf_op jit(solution)/shard_map/encoder/pallas_call | solution.py:407
  55.7 1.7 %copy.13 = bf16[256,512]{1,0:T(8,128)(2,1)} copy(bf16[256,512]{1,0:T(8,128)(2,1)} %encoder.1) | data formatting | bytes 524288

commit v5 on v4

--- a/solution.py
+++ b/solution.py
@@ -38,12 +38,13 @@
 
 
 def gelu(x):
-    u = x * x
-    r = ERF[4]
+    near = x.astype(bf16)
+    u = near * near
+    r = jnp.full_like(u, ERF[4])
     for coefficient in ERF[3::-1]:
-        r = r * u + coefficient
+        r = r * u + jnp.asarray(coefficient, bf16)
     half = 0.5 * x
-    return half + half * jnp.tanh(x * r)
+    return half + half * jnp.tanh((near * r).astype(f32))
 
 
 def norm(x, gain):
@@ -236,6 +237,8 @@
     rim_send_sem,
     rim_recv_sem,
     load_sem,
+    most,
+    rest,
 ):
     loads = [
         pltpu.make_async_copy(src, dst, load_sem.at[n])
@@ -376,15 +379,21 @@
         mean = total / jnp.concatenate([count, count], axis=1)
         return gelu(dot(mean.astype(bf16), wpool[...])).astype(bf16)
 
-    out[...] = pooled(sums[:CELL_DEV, :], counts[:CELL_DEV, :])
+    tail = CELL_DEV - 16
+    most[...] = pooled(sums[:tail, :], counts[:tail, :])
+    store_most = pltpu.make_async_copy(most, out.at[pl.ds(0, tail)], load_sem.at[0])
+    store_most.start()
     rim.wait()
-    tail = CELL_DEV - 16
     last = lax.broadcasted_iota(jnp.int32, (16, 1), 0) == 15
     extra = jnp.where(last, rim_recv[0:1, 0:C], 0.0)
     extra_count = jnp.where(last, rim_recv[0:1, C : C + 128], 0.0)
-    out[tail:, :] = pooled(
+    rest[...] = pooled(
         sums[tail:CELL_DEV, :] + extra, counts[tail:CELL_DEV, :] + extra_count
     )
+    store_rest = pltpu.make_async_copy(rest, out.at[pl.ds(tail, 16)], load_sem.at[1])
+    store_rest.start()
+    store_rest.wait()
+    store_most.wait()
 
 
 def on_device(
@@ -402,13 +411,12 @@
     n_pts = lax.axis_size("pts")
     devices = lax.axis_size(("grp", "pts"))
     deltas = (3, -3, 2, -2, 1, -1, devices // 2, 0)
-    vmem = pl.BlockSpec(memory_space=pltpu.VMEM)
     smem = pl.BlockSpec(memory_space=pltpu.SMEM)
     return pl.pallas_call(
         functools.partial(body, deltas, devices, n_pts),
         out_shape=jax.ShapeDtypeStruct((CELL_DEV, CP), bf16),
         in_specs=[smem, smem] + [pl.BlockSpec(memory_space=pl.ANY)] * 8,
-        out_specs=vmem,
+        out_specs=pl.BlockSpec(memory_space=pl.ANY),
         scratch_shapes=[
             pltpu.VMEM((NB, BLK, C), bf16),
             pltpu.VMEM((NB, BLK), jnp.int32),
@@ -445,6 +453,8 @@
             pltpu.SemaphoreType.DMA,
             pltpu.SemaphoreType.DMA,
             pltpu.SemaphoreType.DMA((8,)),
+            pltpu.VMEM((CELL_DEV - 16, CP), bf16),
+            pltpu.VMEM((16, CP), bf16),
         ],
         compiler_params=pltpu.CompilerParams(
             collective_id=0, has_side_effects=True, vmem_limit_bytes=60 * 2**20

time: 57.6 us -> 56.9 us (0.988)
  Pallas kernels: 55.1 us -> 54.4 us
    pallas_call x1, Pallas kernels: 55.1 us -> 54.4 us  [on_device(): pl.pallas_call(functools.partial(body, deltas, devices, n_pts), out_shape...]
where the time goes in v5:
time: 56.9 us; the launch traced here: 56.8 us
  Pallas kernels  54.4 us (96%)
  local copies, waits for them, and re-layouts  1.67 us (3%)
  between operations  0.66 us (1%)
    pallas_call x1, Pallas kernels, on_device(): pl.pallas_call(functools.partial(body, deltas, devices, n_pts), out_shape...  54.4 us
    unnamed x1, local copies, waits for them, and re-layouts  1.67 us

profile of v5, /device:TPU:1, one launch (start us, length us, event | category | flops | bytes accessed | tf_op | source)
XLA Modules:
  0.0 56.8 jit_solution(13626746151636551749)
XLA Ops:
  0.7 54.4 %encoder.1 = bf16[256,512]{1,0:T(8,128)(2,1)} custom-call(s32[1]{0:T(128)S(6)} %copy.12.patch_len, s32[8]{0:T(128)} %z_dest.1, bf16[8,128,256]{2,1,0:T(8,128)(2,1)} %bitcast.2, s32[8,128]{1,0:T(8,128)} %bitcast.3, f32[2,2,256]{2,1,0:T(2,128)} %gain_hbm.1, bf16[2,256,768]{2,1,0:T(8,128)(2,1)} %wqkv_hbm.1, bf16[2,256,256]{2,1,0:T(8,128)(2,1)} %wo_hbm.1, ...), custom_call_target="tpu_custom_call" | custom-call | tf_op jit(solution)/shard_map/encoder/pallas_call | solution.py:415
  55.1 1.7 %copy.13 = bf16[256,512]{1,0:T(8,128)(2,1)} copy(bf16[256,512]{1,0:T(8,128)(2,1)} %encoder.1) | data formatting | bytes 524288
